TPU v7x, 256 devices: a whole 4x4x8 slice. The times are simulated.
256 devices in a mesh: space: 32 (over z, x), sample: 8 (over y, core).
Axes of the slice: x: 4, y: 4, z: 8, core: 2. Of those that a mesh axis runs over, the one named last changes fastest.
Arguments:
- crops: bfloat16 [256, 16, 64, 1024], P('sample', None, 'space'), may hold values from -6 to 6
- first_kernel: bfloat16 [32, 16, 3, 3, 3], replicated, may hold values from -0.3125 to 0.3125
- second_kernel: bfloat16 [64, 32, 3, 3, 3], replicated, may hold values from -0.21875 to 0.21875
- out_grad: bfloat16 [256, 64, 16, 64], P(('sample', 'space')), may hold values from -0.03125 to 0.03125
Outputs:
- features_out: bfloat16 [256, 64, 16, 64], P(('sample', 'space'))
- first_grad: float32 [32, 16, 3, 3, 3], replicated
- second_grad: float32 [64, 32, 3, 3, 3], replicated
All inputs are finite; a program needn't handle non-finite values.
Results may differ from a plain program's by a relative error of at most 0.012.
Values may be sent and summed in bfloat16 or wider, within the bound.
A program may use at most 128 MiB of HBM per device.

v0:
```python
import jax
import jax.numpy as jnp
from jax import lax
from jax.sharding import PartitionSpec as P

HEIGHT = 8
WIDTH = 128


def forward_conv(field, kernel, depth_pad):
    return lax.conv_general_dilated(
        field,
        kernel,
        (2, 2, 2),
        (depth_pad, (1, 0), (1, 0)),
        dimension_numbers=("NCDHW", "OIDHW", "NCDHW"),
        preferred_element_type=jnp.float32,
    )


def kernel_grad(field, cotangent, depth_pad):
    return lax.conv_general_dilated(
        field,
        cotangent,
        (1, 1, 1),
        (depth_pad, (1, 0), (1, 0)),
        rhs_dilation=(2, 2, 2),
        dimension_numbers=("CNDHW", "IODHW", "CNDHW"),
        preferred_element_type=jnp.float32,
    )


def input_grad(cotangent, kernel):
    flipped = kernel[:, :, ::-1, ::-1, ::-1]
    return lax.conv_general_dilated(
        cotangent,
        flipped,
        (1, 1, 1),
        ((1, 2), (1, 2), (1, 2)),
        lhs_dilation=(2, 2, 2),
        dimension_numbers=("NCDHW", "IODHW", "NCDHW"),
        preferred_element_type=jnp.float32,
    )


def silu_slope(value):
    sigma = jax.nn.sigmoid(value)
    return sigma * (1.0 + value * (1.0 - sigma))


def body(crops, first_kernel, second_kernel, out_grad):
    local_samples, channels_in, planes, flat_cells = crops.shape
    whole_input = lax.all_to_all(crops, "space", split_axis=0, concat_axis=2, tiled=True)
    whole_input = whole_input.reshape(
        whole_input.shape[0], channels_in, whole_input.shape[2], HEIGHT, WIDTH
    )
    first_pre = forward_conv(whole_input, first_kernel, (1, 0))
    act_whole = jax.nn.silu(first_pre).astype(jnp.bfloat16)
    sample_count = act_whole.shape[0]
    second_pre = forward_conv(act_whole, second_kernel, (1, 0))
    features_out = second_pre.astype(jnp.bfloat16).reshape(out_grad.shape)
    cotangent = out_grad.reshape(
        sample_count, out_grad.shape[1], out_grad.shape[2], HEIGHT // 4, WIDTH // 4
    )
    second_grad = kernel_grad(act_whole, cotangent, (1, 0))
    act_grad = input_grad(cotangent, second_kernel).astype(jnp.bfloat16)
    pre_grad = (act_grad.astype(jnp.float32) * silu_slope(first_pre)).astype(jnp.bfloat16)
    first_grad = kernel_grad(whole_input, pre_grad, (1, 0))
    flat = jnp.concatenate([first_grad.reshape(-1), second_grad.reshape(-1)])
    flat = lax.psum(flat, ("space", "sample"))
    first_grad = flat[: first_grad.size].reshape(first_grad.shape)
    second_grad = flat[first_grad.size :].reshape(second_grad.shape)
    return (features_out, first_grad, second_grad)


def solution(mesh):
    placed = (P("sample", None, "space", None), P(), P(), P(("sample", "space"), None, None, None))
    return jax.shard_map(
        body,
        mesh=mesh,
        in_specs=placed,
        out_specs=(P(("sample", "space"), None, None, None), P(), P()),
        check_vma=False,
    )
```

profile of v0, /device:TPU:1, one launch (start us, length us, event | category | flops | bytes accessed | tf_op | source)
XLA Modules:
  0.0 600.1 jit_solution(7680147417381081335)
XLA Ops:
  7.2 12.0 %all-to-all-start = ((bf16[32,16,2,1024]{3,2,1,0:T(2,128)(2,1)}), bf16[32,16,2,1024]{3,2,1,0:T(2,128)(2,1)S(1)}, u32[]{:S(2)}, u32[]{:S(2)}) async-start(bf16[32,16,2,1024]{3,2,1,0:T(2,128)(2,1)} %param.4), calls=%async_computation | async-start | bytes 4194304 | tf_op jit(solution)/shard_map/all_to_all | solution.py:53
  20.9 2.5 fusion.19
  23.3 5.4 copy.84
  28.7 38.9 %all-to-all-done = bf16[32,16,2,1024]{3,2,1,0:T(2,128)(2,1)S(1)} async-done(((bf16[32,16,2,1024]{3,2,1,0:T(2,128)(2,1)}), bf16[32,16,2,1024]{3,2,1,0:T(2,128)(2,1)S(1)}, u32[]{:S(2)}, u32[]{:S(2)}) %all-to-all-start) | async-done | bytes 2097184 | tf_op jit(solution)/shard_map/all_to_all | solution.py:53
  69.0 4.9 copy.102
  73.9 5.6 pad.clone
  79.5 32.4 %copy.71 = bf16[16,64,8,1,8,18]{0,4,5,2,1,3:T(8,128)(2,1)} copy(bf16[16,64,8,1,8,18]{1,2,5,4,0,3:T(8,128)(2,1)} %bitcast.50) | data formatting | bytes 4718592 | tf_op jit(solution)/shard_map/conv_general_dilated | solution.py:11
  111.9 3.9 slice.33
  115.8 20.2 %broadcast_select_fusion = (bf16[32,4,8,9,32]{4,2,3,1,0:T(8,128)(2,1)}, bf16[32,4,8,9,32]{4,2,3,1,0:T(8,128)(2,1)}, f32[32,4,8,9,32]{4,2,3,1,0:T(8,128)}) fusion(pred[8,9]{0,1:T(8,128)(4,1)S(1)} %copy-done.4, bf16[32,16,3,3,3]{0,1,4,3,2:T(8,128)(2,1)S(1)} %copy-done.5, bf16[16,64,8,1,7,2]{0,4,5,2,1,3:T(8,128)(2,1)} %slice.33, ...), kind=kOutput, calls=%fused_computation.30 | convolution fusion | flops 241065984 | bytes 4975688 | tf_op jit(solution)/shard_map/conv_general_dilated | solution.py:11
  136.0 2.6 copy.72
  146.2 4.8 copy.85
  151.0 11.8 %fusion.9 = f32[64,32,3,3,3]{0,1,4,3,2:T(8,128)S(1)} fusion(bf16[32,4,1,64,32]{4,0,3,1,2:T(8,128)(2,1)} %slice.40, bf16[1,64,16,2,32]{1,4,3,2,0:T(8,128)(2,1)S(1)} %bitcast.62), kind=kOutput, calls=%fused_computation.16 | convolution fusion | flops 91443200 | bytes 876544 | tf_op jit(solution)/shard_map/conv_general_dilated | solution.py:22
  162.9 12.3 %copy.93 = f32[64,32,3,3,3]{4,3,2,1,0:T(4,128)} copy(f32[64,32,3,3,3]{0,1,4,3,2:T(8,128)S(1)} %fusion.9) | data formatting | bytes 442368 | tf_op jit(solution)/shard_map/conv_general_dilated | solution.py:22
  175.2 11.0 %reshape.48 = f32[55296]{0:T(1024)} reshape(f32[64,32,3,3,3]{4,3,2,1,0:T(4,128)} %copy.93) | data formatting | bytes 442368 | tf_op jit(solution)/shard_map/reshape | solution.py:69
  186.1 34.9 %copy.86 = bf16[1,16,64,8,128]{1,0,4,3,2:T(2,128)(2,1)} copy(bf16[1,16,64,8,128]{4,3,1,2,0:T(8,128)(2,1)S(1)} %bitcast.49) | data formatting | bytes 4194304 | tf_op jit(solution)/shard_map/reshape | solution.py:54
  221.0 4.5 fusion.8
  225.5 89.8 %fusion.11 = f32[32,16,3,3,3]{0,1,4,3,2:T(8,128)} fusion(bf16[1,16,64,8,128]{1,0,4,3,2:T(2,128)(2,1)} %copy.86, bf16[32,4,1,64,32]{4,0,3,1,2:T(8,128)(2,1)S(1)} %fusion.8), kind=kOutput, calls=%fused_computation.18 | convolution fusion | flops 204385280 | bytes 2676736 | tf_op jit(solution)/shard_map/conv_general_dilated | solution.py:22
  315.3 4.4 copy.88
  319.7 2.0 reshape.47
  323.4 3.5 fusion.26
  328.1 239.1 %all-reduce.2.cloned.1.call-done = f32[69120]{0:T(1024)} async-done(((f32[69120]{0:T(1024)}), f32[69120]{0:T(1024)}) %all-reduce.2.cloned.1.call-update) | async-done | bytes 276496 | tf_op jit(solution)/shard_map/psum | solution.py:70
  569.6 2.5 copy.95
  573.1 8.3 %reshape.50 = f32[64,32,3,3,3]{4,3,2,1,0:T(4,128)} reshape(f32[55296]{0:T(1024)S(1)} %slice.42) | data formatting | bytes 442368 | tf_op jit(solution)/shard_map/reshape | solution.py:72
  581.4 11.7 %copy.96 = f32[64,32,3,3,3]{0,1,4,3,2:T(8,128)} copy(f32[64,32,3,3,3]{4,3,2,1,0:T(4,128)} %reshape.50) | data formatting | bytes 442368
  (38 shorter events, 16.7 us)
Async XLA Ops:
  7.2 13.7 %copy-start = (bf16[64,32,3,3,3]{0,1,4,3,2:T(8,128)(2,1)S(1)}, bf16[64,32,3,3,3]{0,1,4,3,2:T(8,128)(2,1)}, u32[]{:S(2)}) copy-start(bf16[64,32,3,3,3]{0,1,4,3,2:T(8,128)(2,1)} %param.6) | copy-start | bytes 331780
  7.2 13.7 %copy-start.3 = (pred[8,10]{0,1:T(8,128)(4,1)S(1)}, pred[8,10]{0,1:T(8,128)(4,1)}, u32[]{:S(2)}) copy-start(pred[8,10]{0,1:T(8,128)(4,1)} %constant.19) | copy-start | bytes 244
  7.2 60.5 %all-to-all-start = ((bf16[32,16,2,1024]{3,2,1,0:T(2,128)(2,1)}), bf16[32,16,2,1024]{3,2,1,0:T(2,128)(2,1)S(1)}, u32[]{:S(2)}, u32[]{:S(2)}) async-start(bf16[32,16,2,1024]{3,2,1,0:T(2,128)(2,1)} %param.4), calls=%async_computation | async-start | bytes 4194304 | tf_op jit(solution)/shard_map/all_to_all | solution.py:53
  19.2 548.0 %all-reduce.2.cloned.1.call-start = ((), (), s32[]{:S(2)}) async-start(), calls=%async_computation.1 | async-start | bytes 557056 | tf_op jit(solution)/shard_map/psum | solution.py:70
  79.5 36.3 %copy-start.4 = (pred[8,9]{0,1:T(8,128)(4,1)S(1)}, pred[8,9]{0,1:T(8,128)(4,1)}, u32[]{:S(2)}) copy-start(pred[8,9]{0,1:T(8,128)(4,1)} %constant.17) | copy-start | bytes 220
  79.5 36.3 %copy-start.5 = (bf16[32,16,3,3,3]{0,1,4,3,2:T(8,128)(2,1)S(1)}, bf16[32,16,3,3,3]{0,1,4,3,2:T(8,128)(2,1)}, u32[]{:S(2)}) copy-start(bf16[32,16,3,3,3]{0,1,4,3,2:T(8,128)(2,1)} %param.5) | copy-start | bytes 82948
  138.6 3.3 copy-start.2
  140.4 1.5 copy-start.1
  141.9 2.7 slice-start
  141.9 2.7 slice-start.1
Sparse Core Ops, SparseCore 0:
  323.5 243.6 all-reduce.1
where the time goes:
time: 607 us; the launch traced here: 600 us
  waiting for transfers between devices  278 us (46%)
  local copies, waits for them, and re-layouts  160 us (26%)
  matrix products  128 us (21%)
  between operations  14.4 us (2%)
  starting transfers between devices  12.1 us (2%)
  other arithmetic  7.78 us (1%)
    psum x1, waiting for transfers between devices, body(): flat = lax.psum(flat, ('space', 'sample'))  239 us
    conv_general_dilated x2, matrix products, kernel_grad(): lax.conv_general_dilated(field, cotangent, (1, 1, 1), (depth_pad, (1, 0),...  102 us
    reshape x2, local copies, waits for them, and re-layouts, body(): whole_input.reshape(whole_input.shape[0], channels_in, whole_input.shape[...  40.5 us
    all_to_all x1, waiting for transfers between devices, body(): lax.all_to_all(crops, 'space', split_axis=0, concat_axis=2, tiled=True)  38.9 us
    conv_general_dilated x2, local copies, waits for them, and re-layouts, forward_conv(): lax.conv_general_dilated(field, kernel, (2, 2, 2), (depth_pad, (1, 0), (1...  36.3 us
    conv_general_dilated x2, matrix products, forward_conv(): lax.conv_general_dilated(field, kernel, (2, 2, 2), (depth_pad, (1, 0), (1...  23.7 us
    unnamed x23, local copies, waits for them, and re-layouts  22.7 us
    conv_general_dilated x2, local copies, waits for them, and re-layouts, kernel_grad(): lax.conv_general_dilated(field, cotangent, (1, 1, 1), (depth_pad, (1, 0),...  16.7 us
  transfers between devices with their start and end apart: 2, of which 2 were waited for; matrix products, arithmetic and copies ran while one was open for 2% of the time, Pallas kernels for 0%

commit v1 on v0

--- a/solution.py
+++ b/solution.py
@@ -67,7 +67,7 @@
     pre_grad = (act_grad.astype(jnp.float32) * silu_slope(first_pre)).astype(jnp.bfloat16)
     first_grad = kernel_grad(whole_input, pre_grad, (1, 0))
     flat = jnp.concatenate([first_grad.reshape(-1), second_grad.reshape(-1)])
-    flat = lax.psum(flat, ("space", "sample"))
+    flat = lax.psum(lax.psum(flat, "space"), "sample")
     first_grad = flat[: first_grad.size].reshape(first_grad.shape)
     second_grad = flat[first_grad.size :].reshape(second_grad.shape)
     return (features_out, first_grad, second_grad)

time: 607 us -> 565 us (0.931)
  waiting for transfers between devices: 278 us -> 238 us
    psum x1 -> x2, waiting for transfers between devices: 239 us -> 199 us  [body(): flat = lax.psum(lax.psum(flat, 'space'), 'sample')]
    unnamed x23 -> x19, local copies, waits for them, and re-layouts: 22.7 us -> 22.3 us
  transfers between devices with their start and end apart: 2 -> 3, of which waited for: 2 -> 3; matrix products, arithmetic and copies ran while one was open for 2% -> 3% of each run, Pallas kernels for 0% -> 0%
where the time goes in v1:
time: 565 us; the launch traced here: 559 us
  waiting for transfers between devices  238 us (42%)
  local copies, waits for them, and re-layouts  161 us (28%)
  matrix products  126 us (22%)
  between operations  14.4 us (3%)
  starting transfers between devices  12.1 us (2%)
  other arithmetic  7.78 us (1%)
    psum x2, waiting for transfers between devices, body(): flat = lax.psum(lax.psum(flat, 'space'), 'sample')  199 us
    conv_general_dilated x2, matrix products, kernel_grad(): lax.conv_general_dilated(field, cotangent, (1, 1, 1), (depth_pad, (1, 0),...  101 us
    reshape x2, local copies, waits for them, and re-layouts, body(): whole_input.reshape(whole_input.shape[0], channels_in, whole_input.shape[...  40.7 us
    all_to_all x1, waiting for transfers between devices, body(): lax.all_to_all(crops, 'space', split_axis=0, concat_axis=2, tiled=True)  39 us
    conv_general_dilated x2, local copies, waits for them, and re-layouts, forward_conv(): lax.conv_general_dilated(field, kernel, (2, 2, 2), (depth_pad, (1, 0), (1...  36.2 us
    unnamed x19, local copies, waits for them, and re-layouts  22.3 us
    conv_general_dilated x2, matrix products, forward_conv(): lax.conv_general_dilated(field, kernel, (2, 2, 2), (depth_pad, (1, 0), (1...  21.9 us
    conv_general_dilated x2, local copies, waits for them, and re-layouts, kernel_grad(): lax.conv_general_dilated(field, cotangent, (1, 1, 1), (depth_pad, (1, 0),...  16.8 us
  transfers between devices with their start and end apart: 3, of which 3 were waited for; matrix products, arithmetic and copies ran while one was open for 3% of the time, Pallas kernels for 0%

profile of v1, /device:TPU:1, one launch (start us, length us, event | category | flops | bytes accessed | tf_op | source)
XLA Modules:
  0.0 558.9 jit_solution(3667440024557366543)
XLA Ops:
  7.2 12.0 %all-to-all-start = ((bf16[32,16,2,1024]{3,2,1,0:T(2,128)(2,1)}), bf16[32,16,2,1024]{3,2,1,0:T(2,128)(2,1)S(1)}, u32[]{:S(2)}, u32[]{:S(2)}) async-start(bf16[32,16,2,1024]{3,2,1,0:T(2,128)(2,1)} %param.4), calls=%async_computation | async-start | bytes 4194304 | tf_op jit(solution)/shard_map/all_to_all | solution.py:53
  20.9 2.5 fusion.19
  23.3 5.4 copy.84
  28.7 39.0 %all-to-all-done = bf16[32,16,2,1024]{3,2,1,0:T(2,128)(2,1)S(1)} async-done(((bf16[32,16,2,1024]{3,2,1,0:T(2,128)(2,1)}), bf16[32,16,2,1024]{3,2,1,0:T(2,128)(2,1)S(1)}, u32[]{:S(2)}, u32[]{:S(2)}) %all-to-all-start) | async-done | bytes 2097184 | tf_op jit(solution)/shard_map/all_to_all | solution.py:53
  69.0 4.9 copy.102
  73.9 5.6 %pad.clone = bf16[16,64,8,1,144]{1,2,4,0,3:T(8,128)(2,1)} pad(bf16[16,64,8,1,128]{1,2,4,0,3:T(8,128)(2,1)} %copy.102, bf16[]{:T(256)} %constant.6), padding=0_0x0_0x0_0x0_0x1_15 | pad | bytes 4456450 | tf_op jit(solution)/shard_map/reshape | solution.py:54
  79.6 32.5 %copy.71 = bf16[16,64,8,1,8,18]{0,4,5,2,1,3:T(8,128)(2,1)} copy(bf16[16,64,8,1,8,18]{1,2,5,4,0,3:T(8,128)(2,1)} %bitcast.50) | data formatting | bytes 4718592 | tf_op jit(solution)/shard_map/conv_general_dilated | solution.py:11
  112.0 3.8 slice.33
  115.8 20.1 %broadcast_select_fusion = (bf16[32,4,8,9,32]{4,2,3,1,0:T(8,128)(2,1)}, bf16[32,4,8,9,32]{4,2,3,1,0:T(8,128)(2,1)}, f32[32,4,8,9,32]{4,2,3,1,0:T(8,128)}) fusion(pred[8,9]{0,1:T(8,128)(4,1)S(1)} %copy-done.2, bf16[32,16,3,3,3]{0,1,4,3,2:T(8,128)(2,1)S(1)} %copy-done.3, bf16[16,64,8,1,7,2]{0,4,5,2,1,3:T(8,128)(2,1)} %slice.33, ...), kind=kOutput, calls=%fused_computation.30 | convolution fusion | flops 241065984 | bytes 4975688 | tf_op jit(solution)/shard_map/conv_general_dilated | solution.py:11
  136.0 2.7 copy.89
  142.1 4.9 copy.85
  146.9 11.8 %fusion.9 = f32[64,32,3,3,3]{0,1,4,3,2:T(8,128)S(1)} fusion(bf16[32,4,1,64,32]{4,0,3,1,2:T(8,128)(2,1)} %slice.40, bf16[1,64,16,2,32]{1,4,3,2,0:T(8,128)(2,1)S(1)} %bitcast.62), kind=kOutput, calls=%fused_computation.16 | convolution fusion | flops 91443200 | bytes 876544 | tf_op jit(solution)/shard_map/conv_general_dilated | solution.py:22
  158.8 12.2 %copy.93 = f32[64,32,3,3,3]{4,3,2,1,0:T(4,128)} copy(f32[64,32,3,3,3]{0,1,4,3,2:T(8,128)S(1)} %fusion.9) | data formatting | bytes 442368 | tf_op jit(solution)/shard_map/conv_general_dilated | solution.py:22
  171.0 11.0 %reshape.48 = f32[55296]{0:T(1024)} reshape(f32[64,32,3,3,3]{4,3,2,1,0:T(4,128)} %copy.93) | data formatting | bytes 442368 | tf_op jit(solution)/shard_map/reshape | solution.py:69
  181.9 35.0 %copy.86 = bf16[1,16,64,8,128]{1,0,4,3,2:T(2,128)(2,1)} copy(bf16[1,16,64,8,128]{4,3,1,2,0:T(8,128)(2,1)S(1)} %bitcast.49) | data formatting | bytes 4194304 | tf_op jit(solution)/shard_map/reshape | solution.py:54
  217.0 4.5 fusion.8
  221.5 89.6 %fusion.11 = f32[32,16,3,3,3]{0,1,4,3,2:T(8,128)} fusion(bf16[1,16,64,8,128]{1,0,4,3,2:T(2,128)(2,1)} %copy.86, bf16[32,4,1,64,32]{4,0,3,1,2:T(8,128)(2,1)S(1)} %fusion.8), kind=kOutput, calls=%fused_computation.18 | convolution fusion | flops 204385280 | bytes 2676736 | tf_op jit(solution)/shard_map/conv_general_dilated | solution.py:22
  311.1 4.6 copy.88
  319.4 2.6 copy.72
  323.9 134.8 %all-reduce.3.cloned.1.call-done = f32[69120]{0:T(1024)} async-done(((f32[69120]{0:T(1024)}), f32[69120]{0:T(1024)}) %all-reduce.3.cloned.1.call-update) | async-done | bytes 276496 | tf_op jit(solution)/shard_map/psum | solution.py:70
  461.8 64.2 %all-reduce.5.cloned.1.call-done = f32[69120]{0:T(1024)} async-done(((f32[69120]{0:T(1024)}), f32[69120]{0:T(1024)}) %all-reduce.5.cloned.1.call-update) | async-done | bytes 276496 | tf_op jit(solution)/shard_map/psum | solution.py:70
  528.4 2.5 copy.95
  531.9 8.3 %reshape.50 = f32[64,32,3,3,3]{4,3,2,1,0:T(4,128)} reshape(f32[55296]{0:T(1024)S(1)} %slice.42) | data formatting | bytes 442368 | tf_op jit(solution)/shard_map/reshape | solution.py:72
  540.2 11.7 %copy.96 = f32[64,32,3,3,3]{0,1,4,3,2:T(8,128)} copy(f32[64,32,3,3,3]{4,3,2,1,0:T(4,128)} %reshape.50) | data formatting | bytes 442368
  (37 shorter events, 18.3 us)
Async XLA Ops:
  7.2 13.7 %copy-start = (bf16[64,32,3,3,3]{0,1,4,3,2:T(8,128)(2,1)S(1)}, bf16[64,32,3,3,3]{0,1,4,3,2:T(8,128)(2,1)}, u32[]{:S(2)}) copy-start(bf16[64,32,3,3,3]{0,1,4,3,2:T(8,128)(2,1)} %param.6) | copy-start | bytes 331780
  7.2 13.7 %copy-start.1 = (pred[8,10]{0,1:T(8,128)(4,1)S(1)}, pred[8,10]{0,1:T(8,128)(4,1)}, u32[]{:S(2)}) copy-start(pred[8,10]{0,1:T(8,128)(4,1)} %constant.19) | copy-start | bytes 244
  7.2 60.5 %all-to-all-start = ((bf16[32,16,2,1024]{3,2,1,0:T(2,128)(2,1)}), bf16[32,16,2,1024]{3,2,1,0:T(2,128)(2,1)S(1)}, u32[]{:S(2)}, u32[]{:S(2)}) async-start(bf16[32,16,2,1024]{3,2,1,0:T(2,128)(2,1)} %param.4), calls=%async_computation | async-start | bytes 4194304 | tf_op jit(solution)/shard_map/all_to_all | solution.py:53
  19.2 439.5 %all-reduce.3.cloned.1.call-start = ((), (), s32[]{:S(2)}) async-start(), calls=%async_computation.1 | async-start | bytes 557056 | tf_op jit(solution)/shard_map/psum | solution.py:70
  79.6 36.3 %copy-start.2 = (pred[8,9]{0,1:T(8,128)(4,1)S(1)}, pred[8,9]{0,1:T(8,128)(4,1)}, u32[]{:S(2)}) copy-start(pred[8,9]{0,1:T(8,128)(4,1)} %constant.17) | copy-start | bytes 220
  79.6 36.3 %copy-start.3 = (bf16[32,16,3,3,3]{0,1,4,3,2:T(8,128)(2,1)S(1)}, bf16[32,16,3,3,3]{0,1,4,3,2:T(8,128)(2,1)}, u32[]{:S(2)}) copy-start(bf16[32,16,3,3,3]{0,1,4,3,2:T(8,128)(2,1)} %param.5) | copy-start | bytes 82948
  135.9 4.5 slice-start
  135.9 4.5 slice-start.1
  319.3 206.7 %all-reduce.5.cloned.1.call-start = ((), (), s32[]{:S(2)}) async-start(), calls=%async_computation.2 | async-start | bytes 557056 | tf_op jit(solution)/shard_map/psum | solution.py:70
Sparse Core Ops, SparseCore 0:
  319.5 139.1 all-reduce.2
  461.0 64.9 all-reduce.4
